TPU v7x, 128 devices: a whole 4x4x4 slice. The times are simulated.
128 devices in a mesh: ctx: 16 (over z, x_lo, core), tp: 8 (over y, x_hi).
Axes of the slice: x: 4 (x_hi: 2, x_lo: 2; x = x_hi * 2 + x_lo), y: 4, z: 4, core: 2. Of those that a mesh axis runs over, the one named last changes fastest.
Arguments:
- projected: bfloat16 [3, 4096, 8192], P(None, 'ctx', 'tp'), may hold values from -6 to 6
- short_taps: float32 [3, 7, 8192], P(None, None, 'tp'), may hold values from -2.4 to 2.4
- range_filter: bfloat16 [64, 1024], P('tp'), may hold values from -0.1875 to 0.1875
- skip_gain: float32 [8192], P('tp'), may hold values from -4 to 4
- out_weight: bfloat16 [8192, 8192], P('ctx', 'tp'), may hold values from -0.0625 to 0.0625
Outputs:
- mixed: bfloat16 [4096, 8192], P('ctx', 'tp')
All inputs are finite; a program needn't handle non-finite values.
Results may differ from a plain program's by a relative error of at most 0.0057.
Values may be sent and summed in bfloat16 or wider, within the bound.
A program may use at most 192 MiB of HBM per device.

v0:
```python
import jax
import jax.numpy as jnp
from jax import lax
from jax.sharding import PartitionSpec as P


def passed_along(block, axis, distance):
    devices = range(lax.axis_size(axis))
    route = [((i - distance) % len(devices), i) for i in devices]
    return lax.ppermute(block, axis, route)


def short_conv(extended, tap_rows, length):
    accumulated = jnp.zeros((length, extended.shape[1]), jnp.float32)
    rim_width = tap_rows.shape[0] - 1
    for lag_index in range(tap_rows.shape[0]):
        window = extended[rim_width - lag_index : rim_width - lag_index + length]
        accumulated = accumulated + tap_rows[lag_index][None, :] * window.astype(jnp.float32)
    return accumulated


def toeplitz_strip(range_filter, length):
    groups, kept = range_filter.shape
    period = kept + 2 * length
    flipped = range_filter[:, ::-1]
    row = jnp.pad(flipped, ((0, 0), (length, period - length - kept)))
    tiled = jnp.tile(row, (1, length + 1))
    start = length - 1
    shifted = tiled[:, start : start + length * (period - 1)].reshape(groups, length, period - 1)
    return shifted[:, :, : kept + length]


def local(projected, short_taps, range_filter, skip_gain, out_weight):
    length = projected.shape[1]
    width_dev = projected.shape[2]
    groups = range_filter.shape[0]
    group_width = width_dev // groups
    rim_width = short_taps.shape[1] - 1
    span_blocks = range_filter.shape[1] // length
    rim_block = passed_along(projected[:, length - rim_width :, :], "ctx", 1)
    extended = jnp.concatenate([rim_block, projected], axis=1)
    query_feat = short_conv(extended[0], short_taps[0], length)
    key_feat = short_conv(extended[1], short_taps[1], length)
    value_feat = short_conv(extended[2], short_taps[2], length)
    mixed_in = (key_feat * value_feat).astype(jnp.bfloat16)
    strip = toeplitz_strip(range_filter, length)
    pieces = [passed_along(mixed_in, "ctx", offset) for offset in range(span_blocks, 0, -1)]
    window = jnp.concatenate(pieces + [mixed_in], axis=0).reshape(-1, groups, group_width)
    toeplitz = jnp.einsum("gam,mgc->agc", strip, window, preferred_element_type=jnp.float32)
    toeplitz = toeplitz.reshape(length, width_dev)
    restored = lax.optimization_barrier(mixed_in).astype(jnp.float32)
    gated_out = (query_feat * (toeplitz + skip_gain[None, :] * restored)).astype(jnp.bfloat16)
    gathered = lax.all_gather(gated_out, "tp", axis=1, tiled=True)
    summed = jnp.dot(
        gathered,
        lax.all_gather(out_weight, "ctx", axis=0, tiled=True),
        preferred_element_type=jnp.float32,
    )
    return summed.astype(jnp.bfloat16)


def solution(mesh):
    placed = (P(None, "ctx", "tp"), P(None, None, "tp"), P("tp", None), P("tp"), P("ctx", "tp"))
    return jax.shard_map(
        local, mesh=mesh, in_specs=placed, out_specs=P("ctx", "tp"), check_vma=False
    )
```

profile of v0, /device:TPU:1, one launch (start us, length us, event | category | flops | bytes accessed | tf_op | source)
XLA Modules:
  0.0 258.7 jit_solution(12750595578099567330)
XLA Ops:
  6.5 0.8 slice.231
  7.4 2.7 %collective-permute-start = (bf16[3,6,1024]{2,1,0:T(8,128)(2,1)S(1)}, bf16[3,6,1024]{2,1,0:T(8,128)(2,1)S(1)}, u32[]{:S(2)}, u32[]{:S(2)}) collective-permute-start(bf16[3,6,1024]{2,1,0:T(8,128)(2,1)S(1)} %slice.231), channel_id=1, source_target_pairs={{120,0},{0,8},{8,16},{16,24},{24,32},{32,40},{40,48},{48,56},{56,6... | collective-permute-start | bytes 110600 | tf_op jit(solution)/shard_map/ppermute | solution.py:10
  10.0 1.4 fusion.59
  11.5 0.8 fusion.60
  12.3 5.2 %fusion.4 = bf16[256,1024]{1,0:T(8,128)(2,1)S(1)} fusion(bf16[3,6,1024]{2,1,0:T(8,128)(2,1)S(1)} %collective-permute-done, bf16[3,256,1024]{2,1,0:T(8,128)(2,1)} %param.5, f32[1024]{0:T(1024)S(1)} %bitcast.144, f32[1024]{0:T(1024)S(1)} %bitcast.143, f32[1024]{0:T(1024)S(1)} %bitcast.131, f32[1024]{0:T(1024)S(1)} %bitcast.132, f32[1024]{0:T(1024)S(1)} %bitcast.133, ...), kind=kLoop, calls=%fused_computation.23 | loop fusion | flops 23592960 | bytes 3239936 | tf_op jit(solution)/shard_map/convert_element_type | solution.py:45
  17.5 1.7 collective-permute-start.1
  19.2 2.8 %collective-permute-start.2 = (bf16[256,1024]{1,0:T(8,128)(2,1)S(1)}, bf16[256,1024]{1,0:T(8,128)(2,1)S(1)}, u32[]{:S(2)}, u32[]{:S(2)}) collective-permute-start(bf16[256,1024]{1,0:T(8,128)(2,1)S(1)} %fusion.4), channel_id=1, source_target_pairs={{104,0},{112,8},{120,16},{0,24},{8,32},{16,40},{24,48},{32,56},{40... | collective-permute-start | bytes 1572872 | tf_op jit(solution)/shard_map/ppermute | solution.py:10
  22.0 0.3 collective-permute-start.3
  22.3 1.6 collective-permute-start.4
  23.9 0.6 rev.3
  24.6 0.4 tile.4
  25.0 3.9 %slice.307 = bf16[8,392960]{1,0:T(8,128)(2,1)} slice(bf16[8,394752]{1,0:T(8,128)(2,1)S(1)} %bitcast.128), slice={[0:8], [255:393215]} | slice | bytes 12574720 | tf_op jit(solution)/shard_map/slice | solution.py:29
  28.9 14.7 %reshape.143 = bf16[3143680]{0:T(1024)(128)(2,1)} reshape(bf16[8,392960]{1,0:T(8,128)(2,1)} %slice.307) | data formatting | bytes 12574720
  43.6 13.7 %reshape.120 = bf16[8,256,1535]{2,1,0:T(8,128)(2,1)} reshape(bf16[3143680]{0:T(1024)(128)(2,1)} %reshape.143) | data formatting | bytes 12574720 | tf_op jit(solution)/shard_map/reshape | solution.py:29
  57.4 0.8 constant_dynamic-update-slice_fusion.4
  58.2 0.9 collective-permute-done.2
  59.1 0.8 constant_dynamic-update-slice_fusion.3
  59.9 0.8 constant_dynamic-update-slice_fusion.2
  60.7 0.9 constant_dynamic-update-slice_fusion.1
  61.6 0.9 constant_dynamic-update-slice_fusion
  62.5 3.0 %copy.8 = bf16[1280,1024]{0,1:T(8,128)(2,1)S(1)} copy(bf16[1280,1024]{1,0:T(8,128)(2,1)} %constant_dynamic-update-slice_fusion) | data formatting | bytes 5242880 | tf_op jit(solution)/shard_map/concatenate | solution.py:48
  65.4 0.0 copy-start.2
  65.5 5.3 %fusion = f32[8,128,256]{2,1,0:T(8,128)} fusion(bf16[1280,8,128]{0,2,1:T(8,128)(2,1)S(1)} %bitcast.129, bf16[8,256,1535]{2,1,0:T(8,128)(2,1)} %reshape.120), kind=kOutput, calls=%fused_computation.17 | convolution fusion | flops 671088640 | bytes 8912896 | tf_op jit(solution)/shard_map/gam,mgc->agc/dot_general | solution.py:49
  70.8 1.7 copy.9
  72.4 0.0 copy-done
  72.5 1.8 fusion.18
  74.3 0.0 all-gather.3.cloned.1.call-update
  74.3 0.0 all-gather.5.cloned.1.call-start
  74.4 0.7 all-gather.5.cloned.1.call-update
  75.1 72.0 %all-gather.3.cloned.1.call-done = bf16[256,8192]{1,0:T(8,128)(2,1)} async-done(((bf16[256,1024]{1,0:T(8,128)(2,1)}), bf16[256,8192]{1,0:T(8,128)(2,1)}) %all-gather.3.cloned.1.call-update) | async-done | bytes 4194320 | tf_op jit(solution)/shard_map/all_gather | solution.py:53
  147.1 92.4 %all-gather.5.cloned.1.call-done = bf16[8192,1024]{1,0:T(8,128)(2,1)} async-done(((bf16[512,1024]{1,0:T(8,128)(2,1)}), bf16[8192,1024]{1,0:T(8,128)(2,1)}) %all-gather.5.cloned.1.call-update) | async-done | bytes 16777232 | tf_op jit(solution)/shard_map/all_gather | solution.py:56
  239.5 12.3 %convolution_convert_fusion = bf16[256,1024]{1,0:T(8,128)(2,1)} fusion(bf16[256,8192]{1,0:T(8,128)(2,1)} %all-gather.3.cloned.1.call-done, bf16[8192,1024]{1,0:T(8,128)(2,1)} %all-gather.5.cloned.1.call-done), kind=kOutput, calls=%fused_computation.19 | convolution fusion | flops 4295229440 | bytes 21495808 | tf_op jit(solution)/shard_map/dot_general | solution.py:54
  (10 shorter events, 0.0 us)
Async XLA Ops:
  6.5 17.4 %copy-start.1 = (bf16[8,1024]{1,0:T(8,128)(2,1)S(1)}, bf16[8,1024]{1,0:T(8,128)(2,1)}, u32[]{:S(2)}) copy-start(bf16[8,1024]{1,0:T(8,128)(2,1)} %param.7) | copy-start | bytes 49156
  6.5 140.6 %all-gather.3.cloned.1.call-start = ((), (), s32[]{:S(2)}) async-start(), calls=%async_computation | async-start | bytes 4718592 | tf_op jit(solution)/shard_map/all_gather | solution.py:53
  7.4 4.9 %collective-permute-start = (bf16[3,6,1024]{2,1,0:T(8,128)(2,1)S(1)}, bf16[3,6,1024]{2,1,0:T(8,128)(2,1)S(1)}, u32[]{:S(2)}, u32[]{:S(2)}) collective-permute-start(bf16[3,6,1024]{2,1,0:T(8,128)(2,1)S(1)} %slice.231), channel_id=1, source_target_pairs={{120,0},{0,8},{8,16},{16,24},{24,32},{32,40},{40,48},{48,56},{56,6... | collective-permute-start | bytes 110600 | tf_op jit(solution)/shard_map/ppermute | solution.py:10
  17.5 39.8 %collective-permute-start.1 = (bf16[256,1024]{1,0:T(8,128)(2,1)S(1)}, bf16[256,1024]{1,0:T(8,128)(2,1)S(1)}, u32[]{:S(2)}, u32[]{:S(2)}) collective-permute-start(bf16[256,1024]{1,0:T(8,128)(2,1)S(1)} %fusion.4), channel_id=1, source_target_pairs={{96,0},{104,8},{112,16},{120,24},{0,32},{8,40},{16,48},{24,56},{32... | collective-permute-start | bytes 1572872 | tf_op jit(solution)/shard_map/ppermute | solution.py:10
  19.2 39.8 %collective-permute-start.2 = (bf16[256,1024]{1,0:T(8,128)(2,1)S(1)}, bf16[256,1024]{1,0:T(8,128)(2,1)S(1)}, u32[]{:S(2)}, u32[]{:S(2)}) collective-permute-start(bf16[256,1024]{1,0:T(8,128)(2,1)S(1)} %fusion.4), channel_id=1, source_target_pairs={{104,0},{112,8},{120,16},{0,24},{8,32},{16,40},{24,48},{32,56},{40... | collective-permute-start | bytes 1572872 | tf_op jit(solution)/shard_map/ppermute | solution.py:10
  22.0 37.8 %collective-permute-start.3 = (bf16[256,1024]{1,0:T(8,128)(2,1)S(1)}, bf16[256,1024]{1,0:T(8,128)(2,1)S(1)}, u32[]{:S(2)}, u32[]{:S(2)}) collective-permute-start(bf16[256,1024]{1,0:T(8,128)(2,1)S(1)} %fusion.4), channel_id=1, source_target_pairs={{112,0},{120,8},{0,16},{8,24},{16,32},{24,40},{32,48},{40,56},{48,... | collective-permute-start | bytes 1572872 | tf_op jit(solution)/shard_map/ppermute | solution.py:10
  22.3 38.4 %collective-permute-start.4 = (bf16[256,1024]{1,0:T(8,128)(2,1)S(1)}, bf16[256,1024]{1,0:T(8,128)(2,1)S(1)}, u32[]{:S(2)}, u32[]{:S(2)}) collective-permute-start(bf16[256,1024]{1,0:T(8,128)(2,1)S(1)} %fusion.4), channel_id=1, source_target_pairs={{120,0},{0,8},{8,16},{16,24},{24,32},{32,40},{40,48},{48,56},{56,6... | collective-permute-start | bytes 1572872 | tf_op jit(solution)/shard_map/ppermute | solution.py:10
  65.4 7.0 %copy-start.2 = (f32[1024]{0:T(1024)S(1)}, f32[1024]{0:T(1024)}, u32[]{:S(2)}) copy-start(f32[1024]{0:T(1024)} %param.8) | copy-start | bytes 12292
  70.8 1.7 copy-start
  74.3 165.1 %all-gather.5.cloned.1.call-start = ((), (), s32[]{:S(2)}) async-start(), calls=%async_computation.1 | async-start | bytes 17825792 | tf_op jit(solution)/shard_map/all_gather | solution.py:56
Sparse Core Ops, SparseCore 0:
  74.5 72.6 all-gather.2
  148.8 90.6 all-gather.4
where the time goes:
time: 259 us
  waiting for transfers between devices  166 us (64%)
  local copies, waits for them, and re-layouts  45.5 us (18%)
  matrix products  17.6 us (7%)
  between operations  13.5 us (5%)
  starting transfers between devices  9.11 us (4%)
  other arithmetic  7.04 us (3%)
    all_gather x1, waiting for transfers between devices, local(): lax.all_gather(out_weight, 'ctx', axis=0, tiled=True)  92.4 us
    all_gather x1, waiting for transfers between devices, local(): gathered = lax.all_gather(gated_out, 'tp', axis=1, tiled=True)  72 us
    unnamed x11, local copies, waits for them, and re-layouts  18.2 us
    reshape x1, local copies, waits for them, and re-layouts, toeplitz_strip(): tiled[:, start:start + length * (period - 1)]  13.7 us
    dot_general x1, matrix products, local(): jnp.dot(gathered, lax.all_gather(out_weight, 'ctx', axis=0, tiled=True),...  12.3 us
    ppermute x5, starting transfers between devices, passed_along(): return lax.ppermute(block, axis, route)  9.06 us
    dot_general x1, matrix products, local(): jnp.einsum('gam,mgc->agc', strip, window, preferred_element_type=jnp.floa...  5.29 us
    convert_element_type x1, other arithmetic, local(): mixed_in = (key_feat * value_feat).astype(jnp.bfloat16)  5.2 us
  transfers between devices with their start and end apart: 7, of which 3 were waited for; matrix products, arithmetic and copies ran while one was open for 15% of the time, Pallas kernels for 0%

commit v1 on v0

--- a/solution.py
+++ b/solution.py
@@ -50,7 +50,9 @@
     toeplitz = toeplitz.reshape(length, width_dev)
     restored = lax.optimization_barrier(mixed_in).astype(jnp.float32)
     gated_out = (query_feat * (toeplitz + skip_gain[None, :] * restored)).astype(jnp.bfloat16)
-    gathered = lax.all_gather(gated_out, "tp", axis=1, tiled=True)
+    gathered = jnp.concatenate(
+        lax.all_to_all(jnp.stack([gated_out] * lax.axis_size("tp")), "tp", 0, 0), axis=1
+    )
     summed = jnp.dot(
         gathered,
         lax.all_gather(out_weight, "ctx", axis=0, tiled=True),

time: 259 us -> 201 us (0.78)
  the two profiles are of different devices: /device:TPU:1 before, /device:TPU:96 now
where the time goes in v1:
time: 201 us; the launch traced here: 200 us
  blocking collectives  81.7 us (41%)
  local copies, waits for them, and re-layouts  48.5 us (24%)
  waiting for transfers between devices  29.1 us (14%)
  matrix products  18.6 us (9%)
  between operations  13.5 us (7%)
  other arithmetic  6.96 us (3%)
    all_to_all x1, blocking collectives, local(): lax.all_to_all(jnp.stack([gated_out] * lax.axis_size('tp')), 'tp', 0, 0)  81.7 us
    ppermute x5, waiting for transfers between devices, passed_along(): return lax.ppermute(block, axis, route)  28.4 us
    unnamed x11, local copies, waits for them, and re-layouts  18.2 us
    reshape x1, local copies, waits for them, and re-layouts, toeplitz_strip(): tiled[:, start:start + length * (period - 1)]  13.7 us
    dot_general x1, matrix products, local(): jnp.dot(gathered, lax.all_gather(out_weight, 'ctx', axis=0, tiled=True),...  12.4 us
    dot_general x1, matrix products, local(): jnp.einsum('gam,mgc->agc', strip, window, preferred_element_type=jnp.floa...  6.23 us
    concatenate x2, local copies, waits for them, and re-layouts, local(): jnp.concatenate(pieces + [mixed_in], axis=0)  5.29 us
    convert_element_type x1, other arithmetic, local(): mixed_in = (key_feat * value_feat).astype(jnp.bfloat16)  5.11 us
  transfers between devices with their start and end apart: 6, of which 3 were waited for; matrix products, arithmetic and copies ran while one was open for 31% of the time, Pallas kernels for 0%

profile of v1, /device:TPU:96, one launch (start us, length us, event | category | flops | bytes accessed | tf_op | source)
XLA Modules:
  0.0 200.0 jit_solution(17628808848456681576)
XLA Ops:
  6.5 0.7 all-gather.2.cloned.1.call-update
  7.3 0.8 slice.231
  8.1 0.1 collective-permute-start
  8.2 1.4 fusion.59
  9.6 0.8 fusion.60
  10.4 2.1 %collective-permute-done = bf16[3,6,1024]{2,1,0:T(8,128)(2,1)S(1)} collective-permute-done((bf16[3,6,1024]{2,1,0:T(8,128)(2,1)S(1)}, bf16[3,6,1024]{2,1,0:T(8,128)(2,1)S(1)}, u32[]{:S(2)}, u32[]{:S(2)}) %collective-permute-start) | collective-permute-done | bytes 36896 | tf_op jit(solution)/shard_map/ppermute | solution.py:10
  12.6 5.1 %fusion.4 = bf16[256,1024]{1,0:T(8,128)(2,1)S(1)} fusion(bf16[3,6,1024]{2,1,0:T(8,128)(2,1)S(1)} %collective-permute-done, bf16[3,256,1024]{2,1,0:T(8,128)(2,1)} %param.5, f32[1024]{0:T(1024)S(1)} %bitcast.148, f32[1024]{0:T(1024)S(1)} %bitcast.147, f32[1024]{0:T(1024)S(1)} %bitcast.135, f32[1024]{0:T(1024)S(1)} %bitcast.136, f32[1024]{0:T(1024)S(1)} %bitcast.137, ...), kind=kLoop, calls=%fused_computation.23 | loop fusion | flops 23592960 | bytes 3239936 | tf_op jit(solution)/shard_map/convert_element_type | solution.py:45
  17.7 1.0 collective-permute-start.1
  18.7 0.0 collective-permute-start.2
  18.7 0.4 collective-permute-start.3
  19.2 0.1 collective-permute-start.4
  19.3 0.6 rev.3
  19.9 0.4 tile.4
  20.3 3.9 %slice.307 = bf16[8,392960]{1,0:T(8,128)(2,1)} slice(bf16[8,394752]{1,0:T(8,128)(2,1)S(1)} %bitcast.131), slice={[0:8], [255:393215]} | slice | bytes 12574720 | tf_op jit(solution)/shard_map/slice | solution.py:29
  24.2 14.7 %reshape.153 = bf16[3143680]{0:T(1024)(128)(2,1)} reshape(bf16[8,392960]{1,0:T(8,128)(2,1)} %slice.307) | data formatting | bytes 12574720
  39.0 13.7 %reshape.128 = bf16[8,256,1535]{2,1,0:T(8,128)(2,1)} reshape(bf16[3143680]{0:T(1024)(128)(2,1)} %reshape.153) | data formatting | bytes 12574720 | tf_op jit(solution)/shard_map/reshape | solution.py:29
  52.7 13.2 %collective-permute-done.1 = bf16[256,1024]{1,0:T(8,128)(2,1)S(1)} collective-permute-done((bf16[256,1024]{1,0:T(8,128)(2,1)S(1)}, bf16[256,1024]{1,0:T(8,128)(2,1)S(1)}, u32[]{:S(2)}, u32[]{:S(2)}) %collective-permute-start.1) | collective-permute-done | bytes 524320 | tf_op jit(solution)/shard_map/ppermute | solution.py:10
  65.9 0.9 constant_dynamic-update-slice_fusion.4
  66.8 13.1 %collective-permute-done.2 = bf16[256,1024]{1,0:T(8,128)(2,1)S(1)} collective-permute-done((bf16[256,1024]{1,0:T(8,128)(2,1)S(1)}, bf16[256,1024]{1,0:T(8,128)(2,1)S(1)}, u32[]{:S(2)}, u32[]{:S(2)}) %collective-permute-start.2) | collective-permute-done | bytes 524320 | tf_op jit(solution)/shard_map/ppermute | solution.py:10
  79.9 0.8 constant_dynamic-update-slice_fusion.3
  80.7 0.8 constant_dynamic-update-slice_fusion.2
  81.5 0.8 constant_dynamic-update-slice_fusion.1
  82.4 0.8 constant_dynamic-update-slice_fusion
  83.2 4.5 %copy.8 = bf16[1280,1024]{0,1:T(8,128)(2,1)} copy(bf16[1280,1024]{1,0:T(8,128)(2,1)} %constant_dynamic-update-slice_fusion) | data formatting | bytes 5242880 | tf_op jit(solution)/shard_map/concatenate | solution.py:48
  87.7 6.2 %fusion = f32[8,128,256]{2,1,0:T(8,128)} fusion(bf16[1280,8,128]{0,2,1:T(8,128)(2,1)} %bitcast.133, bf16[8,256,1535]{2,1,0:T(8,128)(2,1)} %reshape.128), kind=kOutput, calls=%fused_computation.17 | convolution fusion | flops 671088640 | bytes 8912896 | tf_op jit(solution)/shard_map/gam,mgc->agc/dot_general | solution.py:49
  93.9 1.7 copy.9
  95.6 0.1 copy-done
  95.7 1.8 fusion.18
  97.5 1.2 copy.10
  98.8 0.3 stack.2
  99.1 81.7 %all_to_all.5 = bf16[8,256,1024]{1,2,0:T(8,128)(2,1)} all-to-all(bf16[8,256,1024]{1,2,0:T(8,128)(2,1)S(1)} %stack.2), channel_id=1, replica_groups=mesh['ctx'=16,'tp'=8] {'tp'}, dimensions={0} | all-to-all | bytes 8388608 | tf_op jit(solution)/shard_map/all_to_all | solution.py:54
  180.8 12.4 %convolution_convert_fusion = bf16[256,1024]{1,0:T(8,128)(2,1)} fusion(bf16[256,8192]{0,1:T(8,128)(2,1)} %bitcast.132, bf16[8192,1024]{1,0:T(8,128)(2,1)} %all-gather.2.cloned.1.call-done), kind=kOutput, calls=%fused_computation.19 | convolution fusion | flops 4295229440 | bytes 21495808 | tf_op jit(solution)/shard_map/dot_general | solution.py:56
  (10 shorter events, 0.0 us)
Async XLA Ops:
  6.5 12.8 %copy-start.1 = (bf16[8,1024]{1,0:T(8,128)(2,1)S(1)}, bf16[8,1024]{1,0:T(8,128)(2,1)}, u32[]{:S(2)}) copy-start(bf16[8,1024]{1,0:T(8,128)(2,1)} %param.7) | copy-start | bytes 49156
  6.5 174.2 %all-gather.2.cloned.1.call-start = ((), (), s32[]{:S(2)}) async-start(), calls=%async_computation.1 | async-start | bytes 17825792 | tf_op jit(solution)/shard_map/all_gather | solution.py:58
  8.1 4.5 %collective-permute-start = (bf16[3,6,1024]{2,1,0:T(8,128)(2,1)S(1)}, bf16[3,6,1024]{2,1,0:T(8,128)(2,1)S(1)}, u32[]{:S(2)}, u32[]{:S(2)}) collective-permute-start(bf16[3,6,1024]{2,1,0:T(8,128)(2,1)S(1)} %slice.231), channel_id=1, source_target_pairs={{120,0},{0,8},{8,16},{16,24},{24,32},{32,40},{40,48},{48,56},{56,6... | collective-permute-start | bytes 110600 | tf_op jit(solution)/shard_map/ppermute | solution.py:10
  17.7 48.2 %collective-permute-start.1 = (bf16[256,1024]{1,0:T(8,128)(2,1)S(1)}, bf16[256,1024]{1,0:T(8,128)(2,1)S(1)}, u32[]{:S(2)}, u32[]{:S(2)}) collective-permute-start(bf16[256,1024]{1,0:T(8,128)(2,1)S(1)} %fusion.4), channel_id=1, source_target_pairs={{96,0},{104,8},{112,16},{120,24},{0,32},{8,40},{16,48},{24,56},{32... | collective-permute-start | bytes 1572872 | tf_op jit(solution)/shard_map/ppermute | solution.py:10
  18.7 61.1 %collective-permute-start.2 = (bf16[256,1024]{1,0:T(8,128)(2,1)S(1)}, bf16[256,1024]{1,0:T(8,128)(2,1)S(1)}, u32[]{:S(2)}, u32[]{:S(2)}) collective-permute-start(bf16[256,1024]{1,0:T(8,128)(2,1)S(1)} %fusion.4), channel_id=1, source_target_pairs={{104,0},{112,8},{120,16},{0,24},{8,32},{16,40},{24,48},{32,56},{40... | collective-permute-start | bytes 1572872 | tf_op jit(solution)/shard_map/ppermute | solution.py:10
  18.7 62.0 %collective-permute-start.3 = (bf16[256,1024]{1,0:T(8,128)(2,1)S(1)}, bf16[256,1024]{1,0:T(8,128)(2,1)S(1)}, u32[]{:S(2)}, u32[]{:S(2)}) collective-permute-start(bf16[256,1024]{1,0:T(8,128)(2,1)S(1)} %fusion.4), channel_id=1, source_target_pairs={{112,0},{120,8},{0,16},{8,24},{16,32},{24,40},{32,48},{40,56},{48,... | collective-permute-start | bytes 1572872 | tf_op jit(solution)/shard_map/ppermute | solution.py:10
  19.2 62.4 %collective-permute-start.4 = (bf16[256,1024]{1,0:T(8,128)(2,1)S(1)}, bf16[256,1024]{1,0:T(8,128)(2,1)S(1)}, u32[]{:S(2)}, u32[]{:S(2)}) collective-permute-start(bf16[256,1024]{1,0:T(8,128)(2,1)S(1)} %fusion.4), channel_id=1, source_target_pairs={{120,0},{0,8},{8,16},{16,24},{24,32},{32,40},{40,48},{48,56},{56,6... | collective-permute-start | bytes 1572872 | tf_op jit(solution)/shard_map/ppermute | solution.py:10
  87.7 7.9 %copy-start.2 = (f32[1024]{0:T(1024)S(1)}, f32[1024]{0:T(1024)}, u32[]{:S(2)}) copy-start(f32[1024]{0:T(1024)} %param.8) | copy-start | bytes 12292
  93.9 1.8 copy-start
Sparse Core Ops, SparseCore 0:
  9.0 157.2 all-gather.1
